TPU v7x, 512 devices: a whole 4x8x8 slice. The times are simulated.
512 devices in a mesh: depth: 32 (over x, z), rows: 16 (over y, core).
Axes of the slice: x: 4, y: 8, z: 8, core: 2. Of those that a mesh axis runs over, the one named last changes fastest.
Arguments:
- log_density: float32 [128, 2048, 2048], P('depth', 'rows'), may hold values from -6 to 6
Outputs:
- frame: float32 [4, 2048, 32, 64], P(None, 'rows', 'depth')
All inputs are finite; a program needn't handle non-finite values.
Results may differ from a plain program's by a relative error of at most 0.00002.
Values sent between devices are 32-bit elements; how exact they have to be, the bound alone decides.
No kernel may reach another device: no remote copies, remote signals or barrier semaphores. Data moves between devices by JAX's collectives and lax.ppermute only.
A program may use at most 64 MiB of HBM per device.

v0:
```python
import functools

import jax
import jax.numpy as jnp
from jax import lax
from jax.experimental import pallas as pl
from jax.experimental.pallas import tpu as pltpu
from jax.sharding import PartitionSpec as P


RING = 8


def over(nearer, farther):
    return nearer + (1.0 - nearer[3:4]) * farther


def thirds(values):
    high = values.astype(jnp.bfloat16)
    rest = values - high.astype(jnp.float32)
    middle = rest.astype(jnp.bfloat16)
    low = (rest - middle.astype(jnp.float32)).astype(jnp.bfloat16)
    return jnp.concatenate([high, middle, low], axis=1)


def selection_matrix(width, classes):
    each = width // classes
    source = lax.broadcasted_iota(jnp.int32, (width, width), 0)
    column = lax.broadcasted_iota(jnp.int32, (width, width), 1)
    wanted = classes * (column & (each - 1)) + (column >> (each.bit_length() - 1))
    selection = jnp.where(source == wanted, 1.0, 0.0).astype(jnp.bfloat16)
    return jnp.concatenate([selection] * 3, axis=0)


def params(mebibytes):
    return pltpu.CompilerParams(vmem_limit_bytes=mebibytes * 2**20)


def split_kernel(*refs):
    *refs, selection = refs
    count = len(refs) // 3
    width = selection.shape[1]
    each = width // RING

    @pl.when(pl.program_id(0) == 0)
    def _():
        selection[...] = selection_matrix(width, RING)

    for field, out, edge in zip(refs[:count], refs[count : 2 * count], refs[2 * count :]):
        rows, columns = field.shape
        groups = range(columns // width)
        stacked = [thirds(field[:, b * width : (b + 1) * width]) for b in groups]
        sorted_rows = jnp.dot(
            jnp.concatenate(stacked, axis=0), selection[...], preferred_element_type=jnp.float32
        )
        blocks = [sorted_rows[b * rows : (b + 1) * rows] for b in groups]
        lane = lax.broadcasted_iota(jnp.int32, (rows, 4 * each), 1)
        lower, even = lane < 2 * each, (lane & each) == 0
        sides = {}
        for side in range(len(blocks) // 4):
            for half in range(RING // 4):
                tiles = [
                    block[:, half * 4 * each : (half + 1) * 4 * each]
                    for block in blocks[4 * side : 4 * side + 4]
                ]
                for a, b in ((0, 2), (1, 3)):
                    near, far = tiles[a], tiles[b]
                    tiles[a] = jnp.where(lower, near, pltpu.roll(far, 2 * each, 1))
                    tiles[b] = jnp.where(lower, pltpu.roll(near, 2 * each, 1), far)
                for a, b in ((0, 1), (2, 3)):
                    near, far = tiles[a], tiles[b]
                    tiles[a] = jnp.where(even, near, pltpu.roll(far, each, 1))
                    tiles[b] = jnp.where(even, pltpu.roll(near, 3 * each, 1), far)
                for k in range(4):
                    sides[4 * half + k, side] = tiles[k]
        for p in range(RING):
            values = jnp.concatenate([sides[p, side] for side in range(len(blocks) // 4)], axis=1)
            out[p] = values

            @pl.when(pl.program_id(0) == 0)
            def _(values=values, edge=edge, p=p):
                edge[0, p : p + 1] = values[:1]

            @pl.when(pl.program_id(0) == pl.num_programs(0) - 1)
            def _(values=values, edge=edge, p=p):
                edge[1, p : p + 1] = values[rows - 1 :]


def split_classes(field, chosen):
    _, rows, columns = field.shape
    step = min(rows, 64)
    lanes = columns // RING

    def source(i):
        return pl.BlockSpec((None, step, columns), lambda r: (i, r, 0))

    return pl.pallas_call(
        split_kernel,
        grid=(rows // step,),
        in_specs=[source(i) for i in chosen],
        out_specs=[pl.BlockSpec((RING, step, lanes), lambda r: (0, r, 0)) for _ in chosen]
        + [pl.BlockSpec((2, RING, lanes), lambda r: (0, 0, 0)) for _ in chosen],
        out_shape=[jax.ShapeDtypeStruct((RING, rows, lanes), jnp.float32) for _ in chosen]
        + [jax.ShapeDtypeStruct((2, RING, lanes), jnp.float32) for _ in chosen],
        scratch_shapes=[pltpu.VMEM((768, 256), jnp.bfloat16)],
        compiler_params=params(24),
        cost_estimate=pl.CostEstimate(
            flops=len(chosen) * rows * columns * 1536,
            bytes_accessed=len(chosen) * rows * columns * 8,
            transcendentals=0,
        ),
        name="split_classes",
    )(*[field] * len(chosen))


PARTS = 14


def prepare_kernel(extinction, count, *refs):
    own = refs[:count]
    up, down, out = refs[count:]
    _, rows, lanes = own[0].shape
    sub = lax.broadcasted_iota(jnp.int32, (8, lanes), 0)
    lane = lax.broadcasted_iota(jnp.int32, (8, lanes), 1)

    def row_block(block, carry):
        start = pl.multiple_of(block * 8, 8)
        here = pl.ds(start, 8)
        first = block == 0
        final = block == rows // 8 - 1
        row_above = pl.ds(jnp.maximum(start - 1, 0), 1)
        row_below = pl.ds(jnp.minimum(start + 8, rows - 1), 1)
        for p in range(RING):
            column = [field[p, here, :] for field in own]
            clear = jnp.ones((8, lanes), jnp.float32)
            red = green = blue = jnp.zeros((8, lanes), jnp.float32)
            for i, field in enumerate(own):
                s = column[i]
                k = i * RING + p
                above = jnp.where(first, up[k : k + 1, :], field[p, row_above, :])
                below = jnp.where(final, down[k : k + 1, :], field[p, row_below, :])
                above = jnp.where(sub == 0, above, pltpu.roll(s, 1, 0))
                below = jnp.where(sub == 7, below, pltpu.roll(s, 7, 0))
                dy = below - above
                if p > 0:
                    left = field[p - 1, here, :]
                else:
                    left = pltpu.roll(field[RING - 1, here, :], 1, 1)
                    left = jnp.where(lane == 0, 0.0, left)
                if p < RING - 1:
                    right = field[p + 1, here, :]
                else:
                    right = pltpu.roll(field[0, here, :], lanes - 1, 1)
                    right = jnp.where(lane == lanes - 1, 0.0, right)
                dx = right - left
                sloped = 0.168 * dy + 0.224 * dx
                squared = 0.25 * (dy * dy + dx * dx) + 1.0
                root = jnp.exp(0.5 * s)
                square = root * root
                fourth = square * square
                opacity = 1.0 - jnp.exp(-extinction * (square * root))
                weight = clear * opacity
                clear = clear - weight
                if 0 < i < count - 1:
                    dz = column[i + 1] - column[i - 1]
                    weight *= shade(dz, sloped, squared)
                dark = weight / (1.0 + fourth)
                bright = dark * fourth
                glow = weight * jnp.exp(-s * s)
                if 0 < i < count - 1:
                    red += bright
                    green += glow
                    blue += dark
                else:
                    base = 4 if i == 0 else 9
                    out[p, base, here, :] = bright
                    out[p, base + 1, here, :] = glow
                    out[p, base + 2, here, :] = dark
                    out[p, base + 3, here, :] = sloped
                    out[p, base + 4, here, :] = squared
            out[p, 0, here, :] = red
            out[p, 1, here, :] = green
            out[p, 2, here, :] = blue
            out[p, 3, here, :] = 1.0 - clear
        return carry

    lax.fori_loop(0, rows // 8, row_block, 0)


def shade(dz, sloped, squared):
    return 0.3 + jnp.abs(0.21 * dz + sloped) * lax.rsqrt(0.25 * (dz * dz) + squared)


def prepare(extinction, own, up, down):
    ring, rows, lanes = own[0].shape
    cells = ring * rows * lanes
    return pl.pallas_call(
        functools.partial(prepare_kernel, extinction, len(own)),
        in_specs=[pl.BlockSpec(memory_space=pltpu.VMEM)] * (len(own) + 2),
        out_specs=pl.BlockSpec(memory_space=pltpu.VMEM),
        out_shape=jax.ShapeDtypeStruct((ring, PARTS, rows, lanes), jnp.float32),
        compiler_params=params(32),
        cost_estimate=pl.CostEstimate(
            flops=len(own) * cells * 50, bytes_accessed=72 * cells, transcendentals=len(own) * cells * 5
        ),
        name="prepare",
    )(*own, up, down)


def slab_image(parts, second, before, inner, after):
    opening = shade(second - before, parts[7], parts[8])
    closing = shade(after - inner, parts[12], parts[13])
    return [parts[c] + opening * parts[4 + c] + closing * parts[9 + c] for c in range(3)] + [parts[3]]


def finish_kernel(places, parts, second, before, inner, after, out):
    for row in range(0, out.shape[1], 16):
        here = pl.ds(row, min(16, out.shape[1]))
        planes = [field[here] for field in (second, before, inner, after)]
        image = slab_image([parts[c, here] for c in range(PARTS)], *planes)
        for channel in range(4):
            out[channel, here] = image[channel]


def finish(places, slab):
    _, rows, lanes = slab[1].shape
    count = places.shape[0]
    whole = pl.BlockSpec((None, PARTS, rows, lanes), lambda i, place: (place[i], 0, 0, 0))
    plane = pl.BlockSpec((None, rows, lanes), lambda i, place: (place[i], 0, 0))
    cells = count * rows * lanes
    return pl.pallas_call(
        finish_kernel,
        grid_spec=pltpu.PrefetchScalarGridSpec(
            num_scalar_prefetch=1,
            grid=(count,),
            in_specs=[whole] + [plane] * 4,
            out_specs=[pl.BlockSpec((None, 4, rows, lanes), lambda i, place: (i, 0, 0, 0))],
        ),
        out_shape=[jax.ShapeDtypeStruct((count, 4, rows, lanes), jnp.float32)],
        compiler_params=params(12),
        cost_estimate=pl.CostEstimate(flops=cells * 30, bytes_accessed=cells * 88, transcendentals=cells * 2),
        name="finish",
    )(places, *slab)


def hop_kernel(near_own, received, own, out):
    for row in range(0, out.shape[1], 32):
        here = pl.ds(row, min(32, out.shape[1]))
        pair = (own[:, here], received[:, here])
        out[:, here] = over(*pair) if near_own else over(*pair[::-1])


def hop(received, chunks, number, near_own):
    shape = received.shape
    whole = pl.BlockSpec(shape, lambda i: (0, 0, 0))
    return pl.pallas_call(
        functools.partial(hop_kernel, near_own),
        grid=(1,),
        in_specs=[whole, pl.BlockSpec((None, *shape), lambda i: (number, 0, 0, 0))],
        out_specs=whole,
        out_shape=jax.ShapeDtypeStruct(shape, jnp.float32),
        compiler_params=params(8),
        cost_estimate=pl.CostEstimate(flops=received.size * 2, bytes_accessed=received.size * 12, transcendentals=0),
        name="hop_down" if near_own else "hop_up",
    )(received, chunks)


def merge_kernel(upper, own, left, right, *refs):
    *extras, out = refs
    groups, _, rows, quarter = out.shape
    selection = selection_matrix(quarter * groups, groups)
    step = min(rows, 32)
    for start in range(0, rows, step):
        here = pl.ds(start, step)
        image = over(over(left[:, here], own[:, here]), right[:, here])
        extra = extras[0][:, here] + extras[1][:, here] + extras[2][:, here]
        nearer = upper[0] > 0
        near = jnp.where(nearer, extra, image)
        far = jnp.where(nearer, image, extra)
        image = over(near, far)
        stacked = jnp.concatenate([thirds(image[channel]) for channel in range(4)], axis=0)
        sorted_rows = jnp.dot(stacked, selection, preferred_element_type=jnp.float32)
        for channel in range(4):
            for x in range(groups):
                out[x, channel, here] = sorted_rows[
                    channel * step : (channel + 1) * step, x * quarter : (x + 1) * quarter
                ]


def merge(upper, chunks, left, right, extras, groups):
    count, channels, rows, lanes = chunks.shape
    quarter = lanes // groups
    images = [left, right, *extras]

    def spec(shape):
        return pl.BlockSpec(shape, lambda i, upper: (0,) * len(shape))

    own = pl.BlockSpec((None, channels, rows, lanes), lambda i, upper: (count - 1, 0, 0, 0))
    return pl.pallas_call(
        merge_kernel,
        grid_spec=pltpu.PrefetchScalarGridSpec(
            num_scalar_prefetch=1,
            grid=(1,),
            in_specs=[own] + [spec(image.shape) for image in images],
            out_specs=spec((groups, channels, rows, quarter)),
        ),
        out_shape=jax.ShapeDtypeStruct((groups, channels, rows, quarter), jnp.float32),
        compiler_params=params(20),
        cost_estimate=pl.CostEstimate(
            flops=rows * lanes * 80, bytes_accessed=rows * lanes * 128, transcendentals=0
        ),
        name="merge",
    )(upper, chunks, *images)


def gather_ring(slab):
    depth = lax.axis_size("depth")
    index = lax.axis_index("depth")
    place = lax.rem(index, RING)
    last = depth - 1
    top = depth - RING
    half = RING // 2
    upper = place >= half
    send = functools.partial(lax.ppermute, axis_name="depth")

    offsets = jnp.array([half, 3, RING - 3, 2, RING - 2, 1, RING - 1, 0], jnp.int32)
    (chunks,) = finish(lax.rem(place + offsets, RING), slab)
    ups = [(i, i + 1) for i in range(last) if i % RING < half]
    downs = [(i + 1, i) for i in range(last) if (i + 1) % RING >= half]
    left = send(chunks[0], perm=ups)
    right = send(chunks[0], perm=downs)
    ups = [(i, i + 1) for i in range(last)]
    downs = [(i + 1, i) for i in range(last)]
    extras = []
    for step in range(3):
        distance = 3 - step
        ends = (last, top + distance - 1), (0, RING - distance)
        if step == 0:
            extras.append(send(jnp.where(upper, chunks[1], chunks[2]), perm=ends))
        forward = hop(left, chunks, 2 * step + 1, False)
        left = send(forward, perm=ups)
        backward = hop(right, chunks, 2 * step + 2, True)
        right = send(backward, perm=downs)
        if step:
            extras.append(send(jnp.where(upper, forward, backward), perm=ends))

    groups = depth // RING
    quarters = merge(upper.astype(jnp.int32)[None], chunks, left, right, extras, groups)
    rings = [[x * RING + z for x in range(groups)] for z in range(RING)]
    images = lax.all_to_all(quarters, "depth", 0, 0, axis_index_groups=rings, tiled=True)
    total = images[0]
    for x in range(1, groups):
        total = over(total, images[x])
    return total


def neighbours(axis):
    size = lax.axis_size(axis)
    ups = [(i, i + 1) for i in range(size - 1)]
    return ups, [(j, i) for i, j in ups]


def local(log_density):
    slices = log_density.shape[0]
    ups, downs = neighbours("depth")
    first, final, *outer_edges = split_classes(log_density, (0, slices - 1))
    before = lax.ppermute(final, "depth", ups)
    after = lax.ppermute(first, "depth", downs)
    inner = split_classes(log_density, range(1, slices - 1))
    inner, inner_edges = inner[: slices - 2], inner[slices - 2 :]
    edges = [outer_edges[0], *inner_edges, outer_edges[1]]
    slab = [first, *inner, final]
    ups, downs = neighbours("rows")
    up = lax.ppermute(jnp.concatenate([edge[1] for edge in edges]), "rows", ups)
    down = lax.ppermute(jnp.concatenate([edge[0] for edge in edges]), "rows", downs)
    parts = prepare(0.5 / (slices * lax.axis_size("depth")), slab, up, down)
    image = gather_ring([parts, inner[0], before, inner[-1], after])
    return image[:, :, None, :]


def solution(mesh):
    return jax.shard_map(
        local,
        mesh=mesh,
        in_specs=(P("depth", "rows", None),),
        out_specs=P(None, "rows", "depth", None),
        check_vma=False,
    )
```

profile of v0, /device:TPU:48, one launch (start us, length us, event | category | flops | bytes accessed | tf_op | source)
XLA Modules:
  0.0 151.6 jit_solution(14293131167276156515)
XLA Ops:
  0.0 2.2 %copy-done.2 = f32[4,128,2048]{2,1,0:T(8,128)S(1)} copy-done((f32[4,128,2048]{2,1,0:T(8,128)S(1)}, f32[4,128,2048]{2,1,0:T(8,128)}, u32[]{:S(2)}) %copy-start.2) | copy-done | bytes 4194328
  2.2 4.5 %split_classes.2 = (f32[8,128,256]{2,1,0:T(8,128)}, f32[8,128,256]{2,1,0:T(8,128)}, f32[2,8,256]{2,1,0:T(8,128)S(1)}, f32[2,8,256]{2,1,0:T(8,128)S(1)}) custom-call(f32[4,128,2048]{2,1,0:T(8,128)S(1)} %copy-done.2, f32[4,128,2048]{2,1,0:T(8,128)S(1)} %copy-done.2), custom_call_target="tpu_custom_call" | custom-call | flops 805306368 | bytes 4194304 | tf_op jit(solution)/shard_map/split_classes/pallas_call | solution.py:97
  6.7 4.3 %collective-permute-start.2 = (f32[8,128,256]{2,1,0:T(8,128)}, f32[8,128,256]{2,1,0:T(8,128)S(1)}, u32[]{:S(2)}, u32[]{:S(2)}) collective-permute-start(f32[8,128,256]{2,1,0:T(8,128)} %get-tuple-element.16.refs_3_), channel_id=1, source_target_pairs={{0,16},{16,32},{32,48},{48,64},{64,80},{80,96},{96,112},{112,128},... | collective-permute-start | bytes 3145736 | tf_op jit(solution)/shard_map/ppermute | solution.py:367
  11.0 0.0 copy-start.3
  11.1 1.3 collective-permute-start.3
  12.4 3.7 %split_classes.3 = (f32[8,128,256]{2,1,0:T(8,128)S(1)}, f32[8,128,256]{2,1,0:T(8,128)S(1)}, f32[2,8,256]{2,1,0:T(8,128)S(1)}, f32[2,8,256]{2,1,0:T(8,128)S(1)}) custom-call(f32[4,128,2048]{2,1,0:T(8,128)S(1)} %copy-done.2, f32[4,128,2048]{2,1,0:T(8,128)S(1)} %copy-done.2), custom_call_target="tpu_custom_call" | custom-call | flops 805306368 | bytes 4194304 | tf_op jit(solution)/shard_map/split_classes/pallas_call | solution.py:97
  16.1 2.4 %collective-permute-start.1 = (f32[32,256]{1,0:T(8,128)S(1)}, f32[32,256]{1,0:T(8,128)S(1)}, u32[]{:S(2)}, u32[]{:S(2)}) collective-permute-start(f32[32,256]{1,0:T(8,128)S(1)} %pad_maximum_fusion.1), channel_id=1, source_target_pairs={{1,0},{2,1},{3,2},{4,3},{5,4},{6,5},{7,6},{8,7},{9,8},{10,9},{11,1... | collective-permute-start | bytes 98312 | tf_op jit(solution)/shard_map/ppermute | solution.py:375
  18.5 1.9 %collective-permute-start = (f32[32,256]{1,0:T(8,128)S(1)}, f32[32,256]{1,0:T(8,128)S(1)}, u32[]{:S(2)}, u32[]{:S(2)}) collective-permute-start(f32[32,256]{1,0:T(8,128)S(1)} %pad_maximum_fusion), channel_id=1, source_target_pairs={{0,1},{1,2},{2,3},{3,4},{4,5},{5,6},{6,7},{7,8},{8,9},{9,10},{10,1... | collective-permute-start | bytes 98312 | tf_op jit(solution)/shard_map/ppermute | solution.py:374
  20.5 0.0 collective-permute-done.1.refs_5_
  20.5 3.3 %collective-permute-done.refs_4_ = f32[32,256]{1,0:T(8,128)S(1)} collective-permute-done((f32[32,256]{1,0:T(8,128)S(1)}, f32[32,256]{1,0:T(8,128)S(1)}, u32[]{:S(2)}, u32[]{:S(2)}) %collective-permute-start) | collective-permute-done | bytes 32800 | tf_op jit(solution)/shard_map/ppermute | solution.py:374
  23.7 7.9 %prepare.1.parts = f32[8,14,128,256]{3,2,1,0:T(8,128)S(1)} custom-call(f32[8,128,256]{2,1,0:T(8,128)} %get-tuple-element.13.refs_0_, f32[8,128,256]{2,1,0:T(8,128)S(1)} %get-tuple-element.14.refs_1_.second, f32[8,128,256]{2,1,0:T(8,128)S(1)} %get-tuple-element.15.refs_2_.inner, f32[8,128,256]{2,1,0:T(8,128)} %get-tuple-element.16.refs_3_, ...), custom_call_target="tpu_custom_call" | custom-call | flops 52428800 | bytes 18874368 | tf_op jit(solution)/shard_map/prepare/pallas_call | solution.py:197
  31.7 2.0 %collective-permute-done.2.before = f32[8,128,256]{2,1,0:T(8,128)S(1)} collective-permute-done((f32[8,128,256]{2,1,0:T(8,128)}, f32[8,128,256]{2,1,0:T(8,128)S(1)}, u32[]{:S(2)}, u32[]{:S(2)}) %collective-permute-start.2) | collective-permute-done | bytes 1048608 | tf_op jit(solution)/shard_map/ppermute | solution.py:367
  33.7 4.8 %collective-permute-done.3.after = f32[8,128,256]{2,1,0:T(8,128)} collective-permute-done((f32[8,128,256]{2,1,0:T(8,128)}, f32[8,128,256]{2,1,0:T(8,128)}, u32[]{:S(2)}, u32[]{:S(2)}) %collective-permute-start.3) | collective-permute-done | bytes 1048608 | tf_op jit(solution)/shard_map/ppermute | solution.py:368
  38.5 5.0 %finish.1.own = f32[8,4,128,256]{3,2,1,0:T(8,128)S(1)} custom-call(s32[8]{0:T(128)S(1)} %compare_select_fusion.places, f32[8,14,128,256]{3,2,1,0:T(8,128)S(1)} %prepare.1.parts, f32[8,128,256]{2,1,0:T(8,128)S(1)} %get-tuple-element.14.refs_1_.second, f32[8,128,256]{2,1,0:T(8,128)S(1)} %collective-permute-done.2.before, ...), custom_call_target="tpu_custom_call" | custom-call | flops 7864320 | bytes 23068672 | tf_op jit(solution)/shard_map/finish/pallas_call | solution.py:231
  43.5 1.0 fusion
  44.5 0.7 collective-permute-start.8
  45.2 4.3 %collective-permute-start.4 = (f32[4,128,256]{2,1,0:T(8,128)S(1)}, f32[4,128,256]{2,1,0:T(8,128)S(1)}, u32[]{:S(2)}, u32[]{:S(2)}) collective-permute-start(f32[4,128,256]{2,1,0:T(8,128)S(1)} %get-tuple-element.22), channel_id=1, source_target_pairs={{0,16},{16,32},{32,48},{48,64},{128,144},{144,160},{160,176},{176,... | collective-permute-start | bytes 1572872 | tf_op jit(solution)/shard_map/ppermute | solution.py:330
  49.5 0.0 collective-permute-done.8.received
  49.5 0.1 hop_down.3
  49.5 1.3 collective-permute-start.9
  50.8 8.9 %collective-permute-done.4.received = f32[4,128,256]{2,1,0:T(8,128)S(1)} collective-permute-done((f32[4,128,256]{2,1,0:T(8,128)S(1)}, f32[4,128,256]{2,1,0:T(8,128)S(1)}, u32[]{:S(2)}, u32[]{:S(2)}) %collective-permute-start.4) | collective-permute-done | bytes 524320 | tf_op jit(solution)/shard_map/ppermute | solution.py:330
  59.7 0.1 hop_up.3
  59.8 5.5 %collective-permute-start.5 = (f32[4,128,256]{2,1,0:T(8,128)S(1)}, f32[4,128,256]{2,1,0:T(8,128)S(1)}, u32[]{:S(2)}, u32[]{:S(2)}) collective-permute-start(f32[4,128,256]{2,1,0:T(8,128)S(1)} %hop_up.3), channel_id=1, source_target_pairs={{0,16},{16,32},{32,48},{48,64},{64,80},{80,96},{96,112},{112,128},... | collective-permute-start | bytes 1572872 | tf_op jit(solution)/shard_map/ppermute | solution.py:341
  65.3 0.5 collective-permute-done.9.received
  65.8 0.1 hop_down.4
  65.9 1.3 collective-permute-start.10
  67.2 7.6 %collective-permute-done.5.received = f32[4,128,256]{2,1,0:T(8,128)S(1)} collective-permute-done((f32[4,128,256]{2,1,0:T(8,128)S(1)}, f32[4,128,256]{2,1,0:T(8,128)S(1)}, u32[]{:S(2)}, u32[]{:S(2)}) %collective-permute-start.5) | collective-permute-done | bytes 524320 | tf_op jit(solution)/shard_map/ppermute | solution.py:341
  74.8 0.1 hop_up.4
  74.8 4.9 %collective-permute-start.6 = (f32[4,128,256]{2,1,0:T(8,128)S(1)}, f32[4,128,256]{2,1,0:T(8,128)S(1)}, u32[]{:S(2)}, u32[]{:S(2)}) collective-permute-start(f32[4,128,256]{2,1,0:T(8,128)S(1)} %hop_up.4), channel_id=1, source_target_pairs={{0,16},{16,32},{32,48},{48,64},{64,80},{80,96},{96,112},{112,128},... | collective-permute-start | bytes 1572872 | tf_op jit(solution)/shard_map/ppermute | solution.py:341
  79.7 8.9 %collective-permute-start.12 = (f32[4,128,256]{2,1,0:T(8,128)}, f32[4,128,256]{2,1,0:T(8,128)S(1)}, u32[]{:S(2)}, u32[]{:S(2)}) collective-permute-start(f32[4,128,256]{2,1,0:T(8,128)} %get-tuple-element.21), channel_id=1, source_target_pairs={{496,416},{0,80},{497,417},{1,81},{498,418},{2,82},{499,419},{3,83... | collective-permute-start | bytes 1572872 | tf_op jit(solution)/shard_map/ppermute | solution.py:339
  88.6 0.9 broadcast_select_fusion.1
  89.5 1.3 collective-permute-start.13
  90.8 0.0 collective-permute-done.10.received
  90.8 0.1 hop_down.5
  90.9 0.0 collective-permute-done.6.received
  90.9 0.1 hop_up.5
  91.0 0.9 broadcast_select_fusion
  91.9 28.5 %collective-permute-start.14 = (f32[4,128,256]{2,1,0:T(8,128)}, f32[4,128,256]{2,1,0:T(8,128)S(1)}, u32[]{:S(2)}, u32[]{:S(2)}) collective-permute-start(f32[4,128,256]{2,1,0:T(8,128)} %broadcast_select_fusion), channel_id=1, source_target_pairs={{496,384},{0,112},{497,385},{1,113},{498,386},{2,114},{499,387},{3... | collective-permute-start | bytes 1572872 | tf_op jit(solution)/shard_map/ppermute | solution.py:345
  120.3 1.3 collective-permute-start.11
  121.6 5.4 %collective-permute-start.7 = (f32[4,128,256]{2,1,0:T(8,128)S(1)}, f32[4,128,256]{2,1,0:T(8,128)}, u32[]{:S(2)}, u32[]{:S(2)}) collective-permute-start(f32[4,128,256]{2,1,0:T(8,128)S(1)} %hop_up.5), channel_id=1, source_target_pairs={{0,16},{16,32},{32,48},{48,64},{64,80},{80,96},{96,112},{112,128},... | collective-permute-start | bytes 1572872 | tf_op jit(solution)/shard_map/ppermute | solution.py:341
  127.0 0.3 collective-permute-done.14.refs_2_
  127.3 4.1 %collective-permute-done.11.right = f32[4,128,256]{2,1,0:T(8,128)S(1)} collective-permute-done((f32[4,128,256]{2,1,0:T(8,128)S(1)}, f32[4,128,256]{2,1,0:T(8,128)S(1)}, u32[]{:S(2)}, u32[]{:S(2)}) %collective-permute-start.11) | collective-permute-done | bytes 524320 | tf_op jit(solution)/shard_map/ppermute | solution.py:343
  131.4 1.5 collective-permute-done.7.left
  132.9 2.2 %copy-done.1 = f32[8,4,128,256]{3,2,1,0:T(8,128)S(1)} copy-done((f32[8,4,128,256]{3,2,1,0:T(8,128)S(1)}, f32[8,4,128,256]{3,2,1,0:T(8,128)}, u32[]{:S(2)}) %copy-start.1) | copy-done | bytes 4194328
  135.1 1.6 %merge.1 = f32[4,4,128,64]{3,2,1,0:T(8,128)S(1)} custom-call(s32[1]{0:T(128)} %bitcast.upper, f32[8,4,128,256]{3,2,1,0:T(8,128)S(1)} %copy-done.1, f32[4,128,256]{2,1,0:T(8,128)} %collective-permute-done.7.left, f32[4,128,256]{2,1,0:T(8,128)S(1)} %collective-permute-done.11.right, f32[4,128,256]{2,1,0:T(8,128)S(1)} %collective-permute-done.12.refs_0_, ...), custom_call_target="tpu_custom_call" | custom-call | flops 2621440 | bytes 4194304 | tf_op jit(solution)/shard_map/merge/pallas_call | solution.py:299
  136.7 0.3 copy.4
  137.0 13.8 %all_to_all.5 = f32[4,4,128,64]{2,3,1,0:T(8,128)S(1)} all-to-all(f32[4,4,128,64]{2,3,1,0:T(8,128)S(1)} %copy.4), channel_id=1, replica_groups={{0,128,256,384},{16,144,272,400},{32,160,288,416},{48,176,304,432},{64,..., dimensions={0} | all-to-all | bytes 1048576 | tf_op jit(solution)/shard_map/all_to_all | solution.py:350
  150.9 0.7 fusion.3
  (17 shorter events, 0.1 us)
Async XLA Ops:
  0.0 2.2 %copy-start.2 = (f32[4,128,2048]{2,1,0:T(8,128)S(1)}, f32[4,128,2048]{2,1,0:T(8,128)}, u32[]{:S(2)}) copy-start(f32[4,128,2048]{2,1,0:T(8,128)} %refs_1_.3) | copy-start | bytes 12582916
  6.7 27.0 %collective-permute-start.2 = (f32[8,128,256]{2,1,0:T(8,128)}, f32[8,128,256]{2,1,0:T(8,128)S(1)}, u32[]{:S(2)}, u32[]{:S(2)}) collective-permute-start(f32[8,128,256]{2,1,0:T(8,128)} %get-tuple-element.16.refs_3_), channel_id=1, source_target_pairs={{0,16},{16,32},{32,48},{48,64},{64,80},{80,96},{96,112},{112,128},... | collective-permute-start | bytes 3145736 | tf_op jit(solution)/shard_map/ppermute | solution.py:367
  11.0 9.4 %copy-start.3 = (s32[8]{0:T(128)S(1)}, s32[8]{0:T(128)}, u32[]{:S(2)}) copy-start(s32[8]{0:T(128)} %constant.20.clone) | copy-start | bytes 100
  11.1 27.4 %collective-permute-start.3 = (f32[8,128,256]{2,1,0:T(8,128)}, f32[8,128,256]{2,1,0:T(8,128)}, u32[]{:S(2)}, u32[]{:S(2)}) collective-permute-start(f32[8,128,256]{2,1,0:T(8,128)} %get-tuple-element.13.refs_0_), channel_id=1, source_target_pairs={{16,0},{32,16},{48,32},{64,48},{80,64},{96,80},{112,96},{128,112},... | collective-permute-start | bytes 3145736 | tf_op jit(solution)/shard_map/ppermute | solution.py:368
  16.1 4.4 %collective-permute-start.1 = (f32[32,256]{1,0:T(8,128)S(1)}, f32[32,256]{1,0:T(8,128)S(1)}, u32[]{:S(2)}, u32[]{:S(2)}) collective-permute-start(f32[32,256]{1,0:T(8,128)S(1)} %pad_maximum_fusion.1), channel_id=1, source_target_pairs={{1,0},{2,1},{3,2},{4,3},{5,4},{6,5},{7,6},{8,7},{9,8},{10,9},{11,1... | collective-permute-start | bytes 98312 | tf_op jit(solution)/shard_map/ppermute | solution.py:375
  18.5 5.2 %collective-permute-start = (f32[32,256]{1,0:T(8,128)S(1)}, f32[32,256]{1,0:T(8,128)S(1)}, u32[]{:S(2)}, u32[]{:S(2)}) collective-permute-start(f32[32,256]{1,0:T(8,128)S(1)} %pad_maximum_fusion), channel_id=1, source_target_pairs={{0,1},{1,2},{2,3},{3,4},{4,5},{5,6},{6,7},{7,8},{8,9},{9,10},{10,1... | collective-permute-start | bytes 98312 | tf_op jit(solution)/shard_map/ppermute | solution.py:374
  43.5 47.4 %copy-start = (f32[8,4,128,256]{3,2,1,0:T(8,128)}, f32[8,4,128,256]{3,2,1,0:T(8,128)S(1)}, u32[]{:S(2)}) copy-start(f32[8,4,128,256]{3,2,1,0:T(8,128)S(1)} %finish.1.own) | copy-start | bytes 12582916
  44.5 5.0 %collective-permute-start.8 = (f32[4,128,256]{2,1,0:T(8,128)S(1)}, f32[4,128,256]{2,1,0:T(8,128)S(1)}, u32[]{:S(2)}, u32[]{:S(2)}) collective-permute-start(f32[4,128,256]{2,1,0:T(8,128)S(1)} %get-tuple-element.22), channel_id=1, source_target_pairs={{64,48},{80,64},{96,80},{112,96},{192,176},{208,192},{224,208},{24... | collective-permute-start | bytes 1572872 | tf_op jit(solution)/shard_map/ppermute | solution.py:331
  45.2 14.6 %collective-permute-start.4 = (f32[4,128,256]{2,1,0:T(8,128)S(1)}, f32[4,128,256]{2,1,0:T(8,128)S(1)}, u32[]{:S(2)}, u32[]{:S(2)}) collective-permute-start(f32[4,128,256]{2,1,0:T(8,128)S(1)} %get-tuple-element.22), channel_id=1, source_target_pairs={{0,16},{16,32},{32,48},{48,64},{128,144},{144,160},{160,176},{176,... | collective-permute-start | bytes 1572872 | tf_op jit(solution)/shard_map/ppermute | solution.py:330
  49.5 16.2 %collective-permute-start.9 = (f32[4,128,256]{2,1,0:T(8,128)S(1)}, f32[4,128,256]{2,1,0:T(8,128)S(1)}, u32[]{:S(2)}, u32[]{:S(2)}) collective-permute-start(f32[4,128,256]{2,1,0:T(8,128)S(1)} %hop_down.3), channel_id=1, source_target_pairs={{16,0},{32,16},{48,32},{64,48},{80,64},{96,80},{112,96},{128,112},... | collective-permute-start | bytes 1572872 | tf_op jit(solution)/shard_map/ppermute | solution.py:343
  59.8 15.0 %collective-permute-start.5 = (f32[4,128,256]{2,1,0:T(8,128)S(1)}, f32[4,128,256]{2,1,0:T(8,128)S(1)}, u32[]{:S(2)}, u32[]{:S(2)}) collective-permute-start(f32[4,128,256]{2,1,0:T(8,128)S(1)} %hop_up.3), channel_id=1, source_target_pairs={{0,16},{16,32},{32,48},{48,64},{64,80},{80,96},{96,112},{112,128},... | collective-permute-start | bytes 1572872 | tf_op jit(solution)/shard_map/ppermute | solution.py:341
  65.9 25.0 %collective-permute-start.10 = (f32[4,128,256]{2,1,0:T(8,128)S(1)}, f32[4,128,256]{2,1,0:T(8,128)S(1)}, u32[]{:S(2)}, u32[]{:S(2)}) collective-permute-start(f32[4,128,256]{2,1,0:T(8,128)S(1)} %hop_down.4), channel_id=1, source_target_pairs={{16,0},{32,16},{48,32},{64,48},{80,64},{96,80},{112,96},{128,112},... | collective-permute-start | bytes 1572872 | tf_op jit(solution)/shard_map/ppermute | solution.py:343
  74.8 16.1 %collective-permute-start.6 = (f32[4,128,256]{2,1,0:T(8,128)S(1)}, f32[4,128,256]{2,1,0:T(8,128)S(1)}, u32[]{:S(2)}, u32[]{:S(2)}) collective-permute-start(f32[4,128,256]{2,1,0:T(8,128)S(1)} %hop_up.4), channel_id=1, source_target_pairs={{0,16},{16,32},{32,48},{48,64},{64,80},{80,96},{96,112},{112,128},... | collective-permute-start | bytes 1572872 | tf_op jit(solution)/shard_map/ppermute | solution.py:341
  79.7 47.3 %collective-permute-start.12 = (f32[4,128,256]{2,1,0:T(8,128)}, f32[4,128,256]{2,1,0:T(8,128)S(1)}, u32[]{:S(2)}, u32[]{:S(2)}) collective-permute-start(f32[4,128,256]{2,1,0:T(8,128)} %get-tuple-element.21), channel_id=1, source_target_pairs={{496,416},{0,80},{497,417},{1,81},{498,418},{2,82},{499,419},{3,83... | collective-permute-start | bytes 1572872 | tf_op jit(solution)/shard_map/ppermute | solution.py:339
  89.5 37.5 %collective-permute-start.13 = (f32[4,128,256]{2,1,0:T(8,128)}, f32[4,128,256]{2,1,0:T(8,128)S(1)}, u32[]{:S(2)}, u32[]{:S(2)}) collective-permute-start(f32[4,128,256]{2,1,0:T(8,128)} %broadcast_select_fusion.1), channel_id=1, source_target_pairs={{496,400},{0,96},{497,401},{1,97},{498,402},{2,98},{499,403},{3,99... | collective-permute-start | bytes 1572872 | tf_op jit(solution)/shard_map/ppermute | solution.py:345
  91.9 35.4 %collective-permute-start.14 = (f32[4,128,256]{2,1,0:T(8,128)}, f32[4,128,256]{2,1,0:T(8,128)S(1)}, u32[]{:S(2)}, u32[]{:S(2)}) collective-permute-start(f32[4,128,256]{2,1,0:T(8,128)} %broadcast_select_fusion), channel_id=1, source_target_pairs={{496,384},{0,112},{497,385},{1,113},{498,386},{2,114},{499,387},{3... | collective-permute-start | bytes 1572872 | tf_op jit(solution)/shard_map/ppermute | solution.py:345
  120.3 11.1 %collective-permute-start.11 = (f32[4,128,256]{2,1,0:T(8,128)S(1)}, f32[4,128,256]{2,1,0:T(8,128)S(1)}, u32[]{:S(2)}, u32[]{:S(2)}) collective-permute-start(f32[4,128,256]{2,1,0:T(8,128)S(1)} %hop_down.5), channel_id=1, source_target_pairs={{16,0},{32,16},{48,32},{64,48},{80,64},{96,80},{112,96},{128,112},... | collective-permute-start | bytes 1572872 | tf_op jit(solution)/shard_map/ppermute | solution.py:343
  121.6 11.2 %collective-permute-start.7 = (f32[4,128,256]{2,1,0:T(8,128)S(1)}, f32[4,128,256]{2,1,0:T(8,128)}, u32[]{:S(2)}, u32[]{:S(2)}) collective-permute-start(f32[4,128,256]{2,1,0:T(8,128)S(1)} %hop_up.5), channel_id=1, source_target_pairs={{0,16},{16,32},{32,48},{48,64},{64,80},{80,96},{96,112},{112,128},... | collective-permute-start | bytes 1572872 | tf_op jit(solution)/shard_map/ppermute | solution.py:341
  132.9 2.2 %copy-start.1 = (f32[8,4,128,256]{3,2,1,0:T(8,128)S(1)}, f32[8,4,128,256]{3,2,1,0:T(8,128)}, u32[]{:S(2)}) copy-start(f32[8,4,128,256]{3,2,1,0:T(8,128)} %copy-done) | copy-start | bytes 12582916
where the time goes:
time: 152 us
  starting transfers between devices  73.3 us (48%)
  waiting for transfers between devices  32.9 us (22%)
  Pallas kernels  23.1 us (15%)
  blocking collectives  13.8 us (9%)
  local copies, waits for them, and re-layouts  4.72 us (3%)
  other arithmetic  3.49 us (2%)
    ppermute x2, starting transfers between devices, gather_ring(): extras.append(send(jnp.where(upper, forward, backward), perm=ends))  29.8 us
    ppermute x3, starting transfers between devices, gather_ring(): left = send(forward, perm=ups)  15.8 us
    all_to_all x1, blocking collectives, gather_ring(): lax.all_to_all(quarters, 'depth', 0, 0, axis_index_groups=rings, tiled=True)  13.8 us
    ppermute x3, waiting for transfers between devices, gather_ring(): left = send(forward, perm=ups)  9.07 us
    ppermute x1, waiting for transfers between devices, gather_ring(): left = send(chunks[0], perm=ups)  8.9 us
    ppermute x1, starting transfers between devices, gather_ring(): extras.append(send(jnp.where(upper, chunks[1], chunks[2]), perm=ends))  8.88 us
    pallas_call x2, Pallas kernels, split_classes(): pl.pallas_call(split_kernel, grid=(rows // step,), in_specs=[source(i) fo...  8.17 us
    pallas_call x1, Pallas kernels, prepare(): pl.pallas_call(functools.partial(prepare_kernel, extinction, len(own)), i...  7.94 us
  transfers between devices with their start and end apart: 15, of which 9 were waited for; matrix products, arithmetic and copies ran while one was open for 1% of the time, Pallas kernels for 8%

commit v1 on v0

--- a/solution.py
+++ b/solution.py
@@ -288,14 +288,14 @@
 
 
 def merge(upper, chunks, left, right, extras, groups):
-    count, channels, rows, lanes = chunks.shape
+    channels, rows, lanes = chunks.shape
     quarter = lanes // groups
     images = [left, right, *extras]
 
     def spec(shape):
         return pl.BlockSpec(shape, lambda i, upper: (0,) * len(shape))
 
-    own = pl.BlockSpec((None, channels, rows, lanes), lambda i, upper: (count - 1, 0, 0, 0))
+    own = spec((channels, rows, lanes))
     return pl.pallas_call(
         merge_kernel,
         grid_spec=pltpu.PrefetchScalarGridSpec(
@@ -327,6 +327,7 @@
     (chunks,) = finish(lax.rem(place + offsets, RING), slab)
     ups = [(i, i + 1) for i in range(last) if i % RING < half]
     downs = [(i + 1, i) for i in range(last) if (i + 1) % RING >= half]
+    own = lax.optimization_barrier(chunks[RING - 1])
     left = send(chunks[0], perm=ups)
     right = send(chunks[0], perm=downs)
     ups = [(i, i + 1) for i in range(last)]
@@ -345,7 +346,7 @@
             extras.append(send(jnp.where(upper, forward, backward), perm=ends))
 
     groups = depth // RING
-    quarters = merge(upper.astype(jnp.int32)[None], chunks, left, right, extras, groups)
+    quarters = merge(upper.astype(jnp.int32)[None], own, left, right, extras, groups)
     rings = [[x * RING + z for x in range(groups)] for z in range(RING)]
     images = lax.all_to_all(quarters, "depth", 0, 0, axis_index_groups=rings, tiled=True)
     total = images[0]
@@ -363,6 +364,7 @@
 def local(log_density):
     slices = log_density.shape[0]
     ups, downs = neighbours("depth")
+    log_density = pltpu.with_memory_space_constraint(log_density, pltpu.HBM)
     first, final, *outer_edges = split_classes(log_density, (0, slices - 1))
     before = lax.ppermute(final, "depth", ups)
     after = lax.ppermute(first, "depth", downs)

time: 152 us -> 149 us (0.980)
  local copies, waits for them, and re-layouts: 4.72 us -> 0.34 us
  Pallas kernels: 23.1 us -> 25.7 us
    unnamed x8 -> x2, local copies, waits for them, and re-layouts: 4.39 us -> 0.01 us
    pallas_call x2, Pallas kernels: 8.17 us -> 10.6 us  [split_classes(): pl.pallas_call(split_kernel, grid=(rows // step,), in_specs=[source(i) fo...]
  transfers between devices with their start and end apart: 15 -> 15, of which waited for: 9 -> 9; matrix products, arithmetic and copies ran while one was open for 1% -> 1% of each run, Pallas kernels for 8% -> 9%
where the time goes in v1:
time: 149 us; the launch traced here: 148 us
  starting transfers between devices  73.3 us (49%)
  waiting for transfers between devices  31.7 us (21%)
  Pallas kernels  25.7 us (17%)
  blocking collectives  13.7 us (9%)
  other arithmetic  3.45 us (2%)
    ppermute x2, starting transfers between devices, gather_ring(): extras.append(send(jnp.where(upper, forward, backward), perm=ends))  29.8 us
    ppermute x3, starting transfers between devices, gather_ring(): left = send(forward, perm=ups)  15.8 us
    all_to_all x1, blocking collectives, gather_ring(): lax.all_to_all(quarters, 'depth', 0, 0, axis_index_groups=rings, tiled=True)  13.7 us
    pallas_call x2, Pallas kernels, split_classes(): pl.pallas_call(split_kernel, grid=(rows // step,), in_specs=[source(i) fo...  10.6 us
    ppermute x3, waiting for transfers between devices, gather_ring(): left = send(forward, perm=ups)  8.97 us
    ppermute x1, waiting for transfers between devices, gather_ring(): left = send(chunks[0], perm=ups)  8.9 us
    ppermute x1, starting transfers between devices, gather_ring(): extras.append(send(jnp.where(upper, chunks[1], chunks[2]), perm=ends))  8.88 us
    pallas_call x1, Pallas kernels, prepare(): pl.pallas_call(functools.partial(prepare_kernel, extinction, len(own)), i...  7.94 us
  transfers between devices with their start and end apart: 15, of which 9 were waited for; matrix products, arithmetic and copies ran while one was open for 1% of the time, Pallas kernels for 9%

profile of v1, /device:TPU:48, one launch (start us, length us, event | category | flops | bytes accessed | tf_op | source)
XLA Modules:
  0.0 148.5 jit_solution(6407728422019742977)
XLA Ops:
  0.0 5.7 %split_classes.2 = (f32[8,128,256]{2,1,0:T(8,128)}, f32[8,128,256]{2,1,0:T(8,128)}, f32[2,8,256]{2,1,0:T(8,128)S(1)}, f32[2,8,256]{2,1,0:T(8,128)S(1)}) custom-call(f32[4,128,2048]{2,1,0:T(8,128)} %refs_1_.3, f32[4,128,2048]{2,1,0:T(8,128)} %refs_1_.3), custom_call_target="tpu_custom_call" | custom-call | flops 805306368 | bytes 4194304 | tf_op jit(solution)/shard_map/split_classes/pallas_call | solution.py:97
  5.7 4.3 %collective-permute-start.2 = (f32[8,128,256]{2,1,0:T(8,128)}, f32[8,128,256]{2,1,0:T(8,128)S(1)}, u32[]{:S(2)}, u32[]{:S(2)}) collective-permute-start(f32[8,128,256]{2,1,0:T(8,128)} %get-tuple-element.16.refs_3_), channel_id=1, source_target_pairs={{0,16},{16,32},{32,48},{48,64},{64,80},{80,96},{96,112},{112,128},... | collective-permute-start | bytes 3145736 | tf_op jit(solution)/shard_map/ppermute | solution.py:369
  10.1 0.0 copy-start
  10.1 1.3 collective-permute-start.3
  11.4 4.9 %split_classes.3 = (f32[8,128,256]{2,1,0:T(8,128)S(1)}, f32[8,128,256]{2,1,0:T(8,128)S(1)}, f32[2,8,256]{2,1,0:T(8,128)S(1)}, f32[2,8,256]{2,1,0:T(8,128)S(1)}) custom-call(f32[4,128,2048]{2,1,0:T(8,128)} %refs_1_.3, f32[4,128,2048]{2,1,0:T(8,128)} %refs_1_.3), custom_call_target="tpu_custom_call" | custom-call | flops 805306368 | bytes 4194304 | tf_op jit(solution)/shard_map/split_classes/pallas_call | solution.py:97
  16.3 2.4 %collective-permute-start.1 = (f32[32,256]{1,0:T(8,128)S(1)}, f32[32,256]{1,0:T(8,128)S(1)}, u32[]{:S(2)}, u32[]{:S(2)}) collective-permute-start(f32[32,256]{1,0:T(8,128)S(1)} %pad_maximum_fusion.1), channel_id=1, source_target_pairs={{1,0},{2,1},{3,2},{4,3},{5,4},{6,5},{7,6},{8,7},{9,8},{10,9},{11,1... | collective-permute-start | bytes 98312 | tf_op jit(solution)/shard_map/ppermute | solution.py:377
  18.7 1.9 %collective-permute-start = (f32[32,256]{1,0:T(8,128)S(1)}, f32[32,256]{1,0:T(8,128)S(1)}, u32[]{:S(2)}, u32[]{:S(2)}) collective-permute-start(f32[32,256]{1,0:T(8,128)S(1)} %pad_maximum_fusion), channel_id=1, source_target_pairs={{0,1},{1,2},{2,3},{3,4},{4,5},{5,6},{6,7},{7,8},{8,9},{9,10},{10,1... | collective-permute-start | bytes 98312 | tf_op jit(solution)/shard_map/ppermute | solution.py:376
  20.7 0.0 collective-permute-done.1.refs_5_
  20.7 3.3 %collective-permute-done.refs_4_ = f32[32,256]{1,0:T(8,128)S(1)} collective-permute-done((f32[32,256]{1,0:T(8,128)S(1)}, f32[32,256]{1,0:T(8,128)S(1)}, u32[]{:S(2)}, u32[]{:S(2)}) %collective-permute-start) | collective-permute-done | bytes 32800 | tf_op jit(solution)/shard_map/ppermute | solution.py:376
  24.0 7.9 %prepare.1.parts = f32[8,14,128,256]{3,2,1,0:T(8,128)S(1)} custom-call(f32[8,128,256]{2,1,0:T(8,128)} %get-tuple-element.13.refs_0_, f32[8,128,256]{2,1,0:T(8,128)S(1)} %get-tuple-element.14.refs_1_.second, f32[8,128,256]{2,1,0:T(8,128)S(1)} %get-tuple-element.15.refs_2_.inner, f32[8,128,256]{2,1,0:T(8,128)} %get-tuple-element.16.refs_3_, ...), custom_call_target="tpu_custom_call" | custom-call | flops 52428800 | bytes 18874368 | tf_op jit(solution)/shard_map/prepare/pallas_call | solution.py:197
  31.9 0.8 collective-permute-done.2.before
  32.7 4.8 %collective-permute-done.3.after = f32[8,128,256]{2,1,0:T(8,128)} collective-permute-done((f32[8,128,256]{2,1,0:T(8,128)}, f32[8,128,256]{2,1,0:T(8,128)}, u32[]{:S(2)}, u32[]{:S(2)}) %collective-permute-start.3) | collective-permute-done | bytes 1048608 | tf_op jit(solution)/shard_map/ppermute | solution.py:370
  37.5 5.0 %finish.1.own = f32[8,4,128,256]{3,2,1,0:T(8,128)S(1)} custom-call(s32[8]{0:T(128)S(1)} %compare_select_fusion.places, f32[8,14,128,256]{3,2,1,0:T(8,128)S(1)} %prepare.1.parts, f32[8,128,256]{2,1,0:T(8,128)S(1)} %get-tuple-element.14.refs_1_.second, f32[8,128,256]{2,1,0:T(8,128)S(1)} %collective-permute-done.2.before, ...), custom_call_target="tpu_custom_call" | custom-call | flops 7864320 | bytes 23068672 | tf_op jit(solution)/shard_map/finish/pallas_call | solution.py:231
  42.5 0.9 fusion
  43.4 0.7 collective-permute-start.8
  44.1 4.3 %collective-permute-start.4 = (f32[4,128,256]{2,1,0:T(8,128)S(1)}, f32[4,128,256]{2,1,0:T(8,128)S(1)}, u32[]{:S(2)}, u32[]{:S(2)}) collective-permute-start(f32[4,128,256]{2,1,0:T(8,128)S(1)} %get-tuple-element.22), channel_id=1, source_target_pairs={{0,16},{16,32},{32,48},{48,64},{128,144},{144,160},{160,176},{176,... | collective-permute-start | bytes 1572872 | tf_op jit(solution)/shard_map/ppermute | solution.py:331
  48.4 0.0 collective-permute-done.8.received
  48.5 0.1 hop_down.3
  48.5 1.3 collective-permute-start.9
  49.8 8.9 %collective-permute-done.4.received = f32[4,128,256]{2,1,0:T(8,128)S(1)} collective-permute-done((f32[4,128,256]{2,1,0:T(8,128)S(1)}, f32[4,128,256]{2,1,0:T(8,128)S(1)}, u32[]{:S(2)}, u32[]{:S(2)}) %collective-permute-start.4) | collective-permute-done | bytes 524320 | tf_op jit(solution)/shard_map/ppermute | solution.py:331
  58.7 0.1 hop_up.3
  58.8 5.5 %collective-permute-start.5 = (f32[4,128,256]{2,1,0:T(8,128)S(1)}, f32[4,128,256]{2,1,0:T(8,128)S(1)}, u32[]{:S(2)}, u32[]{:S(2)}) collective-permute-start(f32[4,128,256]{2,1,0:T(8,128)S(1)} %hop_up.3), channel_id=1, source_target_pairs={{0,16},{16,32},{32,48},{48,64},{64,80},{80,96},{96,112},{112,128},... | collective-permute-start | bytes 1572872 | tf_op jit(solution)/shard_map/ppermute | solution.py:342
  64.3 0.5 collective-permute-done.9.received
  64.8 0.1 hop_down.4
  64.8 1.3 collective-permute-start.10
  66.1 7.6 %collective-permute-done.5.received = f32[4,128,256]{2,1,0:T(8,128)S(1)} collective-permute-done((f32[4,128,256]{2,1,0:T(8,128)S(1)}, f32[4,128,256]{2,1,0:T(8,128)S(1)}, u32[]{:S(2)}, u32[]{:S(2)}) %collective-permute-start.5) | collective-permute-done | bytes 524320 | tf_op jit(solution)/shard_map/ppermute | solution.py:342
  73.7 0.1 hop_up.4
  73.8 4.9 %collective-permute-start.6 = (f32[4,128,256]{2,1,0:T(8,128)S(1)}, f32[4,128,256]{2,1,0:T(8,128)S(1)}, u32[]{:S(2)}, u32[]{:S(2)}) collective-permute-start(f32[4,128,256]{2,1,0:T(8,128)S(1)} %hop_up.4), channel_id=1, source_target_pairs={{0,16},{16,32},{32,48},{48,64},{64,80},{80,96},{96,112},{112,128},... | collective-permute-start | bytes 1572872 | tf_op jit(solution)/shard_map/ppermute | solution.py:342
  78.7 8.9 %collective-permute-start.12 = (f32[4,128,256]{2,1,0:T(8,128)}, f32[4,128,256]{2,1,0:T(8,128)S(1)}, u32[]{:S(2)}, u32[]{:S(2)}) collective-permute-start(f32[4,128,256]{2,1,0:T(8,128)} %get-tuple-element.21), channel_id=1, source_target_pairs={{496,416},{0,80},{497,417},{1,81},{498,418},{2,82},{499,419},{3,83... | collective-permute-start | bytes 1572872 | tf_op jit(solution)/shard_map/ppermute | solution.py:340
  87.6 0.9 broadcast_select_fusion.1
  88.5 1.3 collective-permute-start.13
  89.8 0.0 collective-permute-done.10.received
  89.8 0.1 hop_down.5
  89.9 0.0 collective-permute-done.6.received
  89.9 0.1 hop_up.5
  90.0 0.9 broadcast_select_fusion
  90.8 28.5 %collective-permute-start.14 = (f32[4,128,256]{2,1,0:T(8,128)}, f32[4,128,256]{2,1,0:T(8,128)S(1)}, u32[]{:S(2)}, u32[]{:S(2)}) collective-permute-start(f32[4,128,256]{2,1,0:T(8,128)} %broadcast_select_fusion), channel_id=1, source_target_pairs={{496,384},{0,112},{497,385},{1,113},{498,386},{2,114},{499,387},{3... | collective-permute-start | bytes 1572872 | tf_op jit(solution)/shard_map/ppermute | solution.py:346
  119.3 1.3 collective-permute-start.11
  120.6 5.4 %collective-permute-start.7 = (f32[4,128,256]{2,1,0:T(8,128)S(1)}, f32[4,128,256]{2,1,0:T(8,128)}, u32[]{:S(2)}, u32[]{:S(2)}) collective-permute-start(f32[4,128,256]{2,1,0:T(8,128)S(1)} %hop_up.5), channel_id=1, source_target_pairs={{0,16},{16,32},{32,48},{48,64},{64,80},{80,96},{96,112},{112,128},... | collective-permute-start | bytes 1572872 | tf_op jit(solution)/shard_map/ppermute | solution.py:342
  126.0 0.0 collective-permute-done.12.refs_0_
  126.0 0.0 collective-permute-done.13.refs_1_
  126.0 0.3 collective-permute-done.14.refs_2_
  126.3 4.2 %collective-permute-done.11.right = f32[4,128,256]{2,1,0:T(8,128)} collective-permute-done((f32[4,128,256]{2,1,0:T(8,128)S(1)}, f32[4,128,256]{2,1,0:T(8,128)}, u32[]{:S(2)}, u32[]{:S(2)}) %collective-permute-start.11) | collective-permute-done | bytes 524320 | tf_op jit(solution)/shard_map/ppermute | solution.py:344
  130.5 1.4 collective-permute-done.7.left
  131.9 1.8 %merge.1 = f32[4,4,128,64]{3,2,1,0:T(8,128)S(1)} custom-call(s32[1]{0:T(128)} %bitcast.upper, f32[4,128,256]{2,1,0:T(8,128)S(1)} %get-tuple-element.23.own, f32[4,128,256]{2,1,0:T(8,128)} %collective-permute-done.7.left, f32[4,128,256]{2,1,0:T(8,128)} %collective-permute-done.11.right, f32[4,128,256]{2,1,0:T(8,128)S(1)} %collective-permute-done.12.refs_0_, ...), custom_call_target="tpu_custom_call" | custom-call | flops 2621440 | bytes 4194304 | tf_op jit(solution)/shard_map/merge/pallas_call | solution.py:299
  133.7 0.3 copy.4
  134.0 13.7 %all_to_all.5 = f32[4,4,128,64]{2,3,1,0:T(8,128)S(1)} all-to-all(f32[4,4,128,64]{2,3,1,0:T(8,128)S(1)} %copy.4), channel_id=1, replica_groups={{0,128,256,384},{16,144,272,400},{32,160,288,416},{48,176,304,432},{64,..., dimensions={0} | all-to-all | bytes 1048576 | tf_op jit(solution)/shard_map/all_to_all | solution.py:351
  147.8 0.7 fusion.3
  (11 shorter events, 0.1 us)
Async XLA Ops:
  5.7 27.0 %collective-permute-start.2 = (f32[8,128,256]{2,1,0:T(8,128)}, f32[8,128,256]{2,1,0:T(8,128)S(1)}, u32[]{:S(2)}, u32[]{:S(2)}) collective-permute-start(f32[8,128,256]{2,1,0:T(8,128)} %get-tuple-element.16.refs_3_), channel_id=1, source_target_pairs={{0,16},{16,32},{32,48},{48,64},{64,80},{80,96},{96,112},{112,128},... | collective-permute-start | bytes 3145736 | tf_op jit(solution)/shard_map/ppermute | solution.py:369
  10.1 10.6 %copy-start = (s32[8]{0:T(128)S(1)}, s32[8]{0:T(128)}, u32[]{:S(2)}) copy-start(s32[8]{0:T(128)} %constant.20.clone) | copy-start | bytes 100
  10.1 27.4 %collective-permute-start.3 = (f32[8,128,256]{2,1,0:T(8,128)}, f32[8,128,256]{2,1,0:T(8,128)}, u32[]{:S(2)}, u32[]{:S(2)}) collective-permute-start(f32[8,128,256]{2,1,0:T(8,128)} %get-tuple-element.13.refs_0_), channel_id=1, source_target_pairs={{16,0},{32,16},{48,32},{64,48},{80,64},{96,80},{112,96},{128,112},... | collective-permute-start | bytes 3145736 | tf_op jit(solution)/shard_map/ppermute | solution.py:370
  16.3 4.4 %collective-permute-start.1 = (f32[32,256]{1,0:T(8,128)S(1)}, f32[32,256]{1,0:T(8,128)S(1)}, u32[]{:S(2)}, u32[]{:S(2)}) collective-permute-start(f32[32,256]{1,0:T(8,128)S(1)} %pad_maximum_fusion.1), channel_id=1, source_target_pairs={{1,0},{2,1},{3,2},{4,3},{5,4},{6,5},{7,6},{8,7},{9,8},{10,9},{11,1... | collective-permute-start | bytes 98312 | tf_op jit(solution)/shard_map/ppermute | solution.py:377
  18.7 5.2 %collective-permute-start = (f32[32,256]{1,0:T(8,128)S(1)}, f32[32,256]{1,0:T(8,128)S(1)}, u32[]{:S(2)}, u32[]{:S(2)}) collective-permute-start(f32[32,256]{1,0:T(8,128)S(1)} %pad_maximum_fusion), channel_id=1, source_target_pairs={{0,1},{1,2},{2,3},{3,4},{4,5},{5,6},{6,7},{7,8},{8,9},{9,10},{10,1... | collective-permute-start | bytes 98312 | tf_op jit(solution)/shard_map/ppermute | solution.py:376
  43.4 5.0 %collective-permute-start.8 = (f32[4,128,256]{2,1,0:T(8,128)S(1)}, f32[4,128,256]{2,1,0:T(8,128)S(1)}, u32[]{:S(2)}, u32[]{:S(2)}) collective-permute-start(f32[4,128,256]{2,1,0:T(8,128)S(1)} %get-tuple-element.22), channel_id=1, source_target_pairs={{64,48},{80,64},{96,80},{112,96},{192,176},{208,192},{224,208},{24... | collective-permute-start | bytes 1572872 | tf_op jit(solution)/shard_map/ppermute | solution.py:332
  44.1 14.6 %collective-permute-start.4 = (f32[4,128,256]{2,1,0:T(8,128)S(1)}, f32[4,128,256]{2,1,0:T(8,128)S(1)}, u32[]{:S(2)}, u32[]{:S(2)}) collective-permute-start(f32[4,128,256]{2,1,0:T(8,128)S(1)} %get-tuple-element.22), channel_id=1, source_target_pairs={{0,16},{16,32},{32,48},{48,64},{128,144},{144,160},{160,176},{176,... | collective-permute-start | bytes 1572872 | tf_op jit(solution)/shard_map/ppermute | solution.py:331
  48.5 16.2 %collective-permute-start.9 = (f32[4,128,256]{2,1,0:T(8,128)S(1)}, f32[4,128,256]{2,1,0:T(8,128)S(1)}, u32[]{:S(2)}, u32[]{:S(2)}) collective-permute-start(f32[4,128,256]{2,1,0:T(8,128)S(1)} %hop_down.3), channel_id=1, source_target_pairs={{16,0},{32,16},{48,32},{64,48},{80,64},{96,80},{112,96},{128,112},... | collective-permute-start | bytes 1572872 | tf_op jit(solution)/shard_map/ppermute | solution.py:344
  58.8 14.9 %collective-permute-start.5 = (f32[4,128,256]{2,1,0:T(8,128)S(1)}, f32[4,128,256]{2,1,0:T(8,128)S(1)}, u32[]{:S(2)}, u32[]{:S(2)}) collective-permute-start(f32[4,128,256]{2,1,0:T(8,128)S(1)} %hop_up.3), channel_id=1, source_target_pairs={{0,16},{16,32},{32,48},{48,64},{64,80},{80,96},{96,112},{112,128},... | collective-permute-start | bytes 1572872 | tf_op jit(solution)/shard_map/ppermute | solution.py:342
  64.8 25.0 %collective-permute-start.10 = (f32[4,128,256]{2,1,0:T(8,128)S(1)}, f32[4,128,256]{2,1,0:T(8,128)S(1)}, u32[]{:S(2)}, u32[]{:S(2)}) collective-permute-start(f32[4,128,256]{2,1,0:T(8,128)S(1)} %hop_down.4), channel_id=1, source_target_pairs={{16,0},{32,16},{48,32},{64,48},{80,64},{96,80},{112,96},{128,112},... | collective-permute-start | bytes 1572872 | tf_op jit(solution)/shard_map/ppermute | solution.py:344
  73.8 16.1 %collective-permute-start.6 = (f32[4,128,256]{2,1,0:T(8,128)S(1)}, f32[4,128,256]{2,1,0:T(8,128)S(1)}, u32[]{:S(2)}, u32[]{:S(2)}) collective-permute-start(f32[4,128,256]{2,1,0:T(8,128)S(1)} %hop_up.4), channel_id=1, source_target_pairs={{0,16},{16,32},{32,48},{48,64},{64,80},{80,96},{96,112},{112,128},... | collective-permute-start | bytes 1572872 | tf_op jit(solution)/shard_map/ppermute | solution.py:342
  78.7 47.3 %collective-permute-start.12 = (f32[4,128,256]{2,1,0:T(8,128)}, f32[4,128,256]{2,1,0:T(8,128)S(1)}, u32[]{:S(2)}, u32[]{:S(2)}) collective-permute-start(f32[4,128,256]{2,1,0:T(8,128)} %get-tuple-element.21), channel_id=1, source_target_pairs={{496,416},{0,80},{497,417},{1,81},{498,418},{2,82},{499,419},{3,83... | collective-permute-start | bytes 1572872 | tf_op jit(solution)/shard_map/ppermute | solution.py:340
  88.5 37.5 %collective-permute-start.13 = (f32[4,128,256]{2,1,0:T(8,128)}, f32[4,128,256]{2,1,0:T(8,128)S(1)}, u32[]{:S(2)}, u32[]{:S(2)}) collective-permute-start(f32[4,128,256]{2,1,0:T(8,128)} %broadcast_select_fusion.1), channel_id=1, source_target_pairs={{496,400},{0,96},{497,401},{1,97},{498,402},{2,98},{499,403},{3,99... | collective-permute-start | bytes 1572872 | tf_op jit(solution)/shard_map/ppermute | solution.py:346
  90.8 35.4 %collective-permute-start.14 = (f32[4,128,256]{2,1,0:T(8,128)}, f32[4,128,256]{2,1,0:T(8,128)S(1)}, u32[]{:S(2)}, u32[]{:S(2)}) collective-permute-start(f32[4,128,256]{2,1,0:T(8,128)} %broadcast_select_fusion), channel_id=1, source_target_pairs={{496,384},{0,112},{497,385},{1,113},{498,386},{2,114},{499,387},{3... | collective-permute-start | bytes 1572872 | tf_op jit(solution)/shard_map/ppermute | solution.py:346
  119.3 11.2 %collective-permute-start.11 = (f32[4,128,256]{2,1,0:T(8,128)S(1)}, f32[4,128,256]{2,1,0:T(8,128)}, u32[]{:S(2)}, u32[]{:S(2)}) collective-permute-start(f32[4,128,256]{2,1,0:T(8,128)S(1)} %hop_down.5), channel_id=1, source_target_pairs={{16,0},{32,16},{48,32},{64,48},{80,64},{96,80},{112,96},{128,112},... | collective-permute-start | bytes 1572872 | tf_op jit(solution)/shard_map/ppermute | solution.py:344
  120.6 11.2 %collective-permute-start.7 = (f32[4,128,256]{2,1,0:T(8,128)S(1)}, f32[4,128,256]{2,1,0:T(8,128)}, u32[]{:S(2)}, u32[]{:S(2)}) collective-permute-start(f32[4,128,256]{2,1,0:T(8,128)S(1)} %hop_up.5), channel_id=1, source_target_pairs={{0,16},{16,32},{32,48},{48,64},{64,80},{80,96},{96,112},{112,128},... | collective-permute-start | bytes 1572872 | tf_op jit(solution)/shard_map/ppermute | solution.py:342

commit v2 on v1

--- a/solution.py
+++ b/solution.py
@@ -313,6 +313,30 @@
     )(upper, chunks, *images)
 
 
+def fold_kernel(images, out):
+    rows = out.shape[1]
+    step = min(rows, 32)
+    for start in range(0, rows, step):
+        here = pl.ds(start, step)
+        total = images[0, :, here]
+        for x in range(1, images.shape[0]):
+            total = over(total, images[x, :, here])
+        out[:, here] = total
+
+
+def fold(images):
+    shape = images.shape[1:]
+    return pl.pallas_call(
+        fold_kernel,
+        grid=(1,),
+        in_specs=[pl.BlockSpec(images.shape, lambda i: (0, 0, 0, 0))],
+        out_specs=pl.BlockSpec(shape, lambda i: (0, 0, 0)),
+        out_shape=jax.ShapeDtypeStruct(shape, jnp.float32),
+        compiler_params=params(12),
+        name="fold",
+    )(images)
+
+
 def gather_ring(slab):
     depth = lax.axis_size("depth")
     index = lax.axis_index("depth")
@@ -349,10 +373,7 @@
     quarters = merge(upper.astype(jnp.int32)[None], own, left, right, extras, groups)
     rings = [[x * RING + z for x in range(groups)] for z in range(RING)]
     images = lax.all_to_all(quarters, "depth", 0, 0, axis_index_groups=rings, tiled=True)
-    total = images[0]
-    for x in range(1, groups):
-        total = over(total, images[x])
-    return total
+    return fold(images)
 
 
 def neighbours(axis):

time: 149 us -> 150 us (level)
  no operation moved by 1% of the time
where the time goes in v2:
time: 150 us; the launch traced here: 149 us
  starting transfers between devices  73.3 us (49%)
  waiting for transfers between devices  31.7 us (21%)
  Pallas kernels  25.7 us (17%)
  blocking collectives  13.7 us (9%)
  other arithmetic  2.72 us (2%)
    ppermute x2, starting transfers between devices, gather_ring(): extras.append(send(jnp.where(upper, forward, backward), perm=ends))  29.8 us
    ppermute x3, starting transfers between devices, gather_ring(): left = send(forward, perm=ups)  15.8 us
    all_to_all x1, blocking collectives, gather_ring(): lax.all_to_all(quarters, 'depth', 0, 0, axis_index_groups=rings, tiled=True)  13.7 us
    pallas_call x2, Pallas kernels, split_classes(): pl.pallas_call(split_kernel, grid=(rows // step,), in_specs=[source(i) fo...  10.6 us
    ppermute x3, waiting for transfers between devices, gather_ring(): left = send(forward, perm=ups)  8.97 us
    ppermute x1, waiting for transfers between devices, gather_ring(): left = send(chunks[0], perm=ups)  8.9 us
    ppermute x1, starting transfers between devices, gather_ring(): extras.append(send(jnp.where(upper, chunks[1], chunks[2]), perm=ends))  8.88 us
    pallas_call x1, Pallas kernels, prepare(): pl.pallas_call(functools.partial(prepare_kernel, extinction, len(own)), i...  7.94 us
  transfers between devices with their start and end apart: 15, of which 9 were waited for; matrix products, arithmetic and copies ran while one was open for 1% of the time, Pallas kernels for 9%

profile of v2, /device:TPU:48, one launch (start us, length us, event | category | flops | bytes accessed | tf_op | source)
XLA Modules:
  0.0 148.9 jit_solution(13595829252628392691)
XLA Ops:
  0.0 5.7 %split_classes.2 = (f32[8,128,256]{2,1,0:T(8,128)}, f32[8,128,256]{2,1,0:T(8,128)}, f32[2,8,256]{2,1,0:T(8,128)S(1)}, f32[2,8,256]{2,1,0:T(8,128)S(1)}) custom-call(f32[4,128,2048]{2,1,0:T(8,128)} %refs_1_.3, f32[4,128,2048]{2,1,0:T(8,128)} %refs_1_.3), custom_call_target="tpu_custom_call" | custom-call | flops 805306368 | bytes 4194304 | tf_op jit(solution)/shard_map/split_classes/pallas_call | solution.py:97
  5.7 4.3 %collective-permute-start.2 = (f32[8,128,256]{2,1,0:T(8,128)}, f32[8,128,256]{2,1,0:T(8,128)S(1)}, u32[]{:S(2)}, u32[]{:S(2)}) collective-permute-start(f32[8,128,256]{2,1,0:T(8,128)} %get-tuple-element.16.refs_3_), channel_id=1, source_target_pairs={{0,16},{16,32},{32,48},{48,64},{64,80},{80,96},{96,112},{112,128},... | collective-permute-start | bytes 3145736 | tf_op jit(solution)/shard_map/ppermute | solution.py:390
  10.1 0.0 copy-start
  10.1 1.3 collective-permute-start.3
  11.4 4.9 %split_classes.3 = (f32[8,128,256]{2,1,0:T(8,128)S(1)}, f32[8,128,256]{2,1,0:T(8,128)S(1)}, f32[2,8,256]{2,1,0:T(8,128)S(1)}, f32[2,8,256]{2,1,0:T(8,128)S(1)}) custom-call(f32[4,128,2048]{2,1,0:T(8,128)} %refs_1_.3, f32[4,128,2048]{2,1,0:T(8,128)} %refs_1_.3), custom_call_target="tpu_custom_call" | custom-call | flops 805306368 | bytes 4194304 | tf_op jit(solution)/shard_map/split_classes/pallas_call | solution.py:97
  16.3 2.4 %collective-permute-start.1 = (f32[32,256]{1,0:T(8,128)S(1)}, f32[32,256]{1,0:T(8,128)S(1)}, u32[]{:S(2)}, u32[]{:S(2)}) collective-permute-start(f32[32,256]{1,0:T(8,128)S(1)} %pad_maximum_fusion.1), channel_id=1, source_target_pairs={{1,0},{2,1},{3,2},{4,3},{5,4},{6,5},{7,6},{8,7},{9,8},{10,9},{11,1... | collective-permute-start | bytes 98312 | tf_op jit(solution)/shard_map/ppermute | solution.py:398
  18.7 1.9 %collective-permute-start = (f32[32,256]{1,0:T(8,128)S(1)}, f32[32,256]{1,0:T(8,128)S(1)}, u32[]{:S(2)}, u32[]{:S(2)}) collective-permute-start(f32[32,256]{1,0:T(8,128)S(1)} %pad_maximum_fusion), channel_id=1, source_target_pairs={{0,1},{1,2},{2,3},{3,4},{4,5},{5,6},{6,7},{7,8},{8,9},{9,10},{10,1... | collective-permute-start | bytes 98312 | tf_op jit(solution)/shard_map/ppermute | solution.py:397
  20.7 0.0 collective-permute-done.1.refs_5_
  20.7 3.3 %collective-permute-done.refs_4_ = f32[32,256]{1,0:T(8,128)S(1)} collective-permute-done((f32[32,256]{1,0:T(8,128)S(1)}, f32[32,256]{1,0:T(8,128)S(1)}, u32[]{:S(2)}, u32[]{:S(2)}) %collective-permute-start) | collective-permute-done | bytes 32800 | tf_op jit(solution)/shard_map/ppermute | solution.py:397
  24.0 7.9 %prepare.1.parts = f32[8,14,128,256]{3,2,1,0:T(8,128)S(1)} custom-call(f32[8,128,256]{2,1,0:T(8,128)} %get-tuple-element.13.refs_0_, f32[8,128,256]{2,1,0:T(8,128)S(1)} %get-tuple-element.14.refs_1_.second, f32[8,128,256]{2,1,0:T(8,128)S(1)} %get-tuple-element.15.refs_2_.inner, f32[8,128,256]{2,1,0:T(8,128)} %get-tuple-element.16.refs_3_, ...), custom_call_target="tpu_custom_call" | custom-call | flops 52428800 | bytes 18874368 | tf_op jit(solution)/shard_map/prepare/pallas_call | solution.py:197
  31.9 0.8 collective-permute-done.2.before
  32.7 4.8 %collective-permute-done.3.after = f32[8,128,256]{2,1,0:T(8,128)} collective-permute-done((f32[8,128,256]{2,1,0:T(8,128)}, f32[8,128,256]{2,1,0:T(8,128)}, u32[]{:S(2)}, u32[]{:S(2)}) %collective-permute-start.3) | collective-permute-done | bytes 1048608 | tf_op jit(solution)/shard_map/ppermute | solution.py:391
  37.5 5.0 %finish.1.own = f32[8,4,128,256]{3,2,1,0:T(8,128)S(1)} custom-call(s32[8]{0:T(128)S(1)} %compare_select_fusion.places, f32[8,14,128,256]{3,2,1,0:T(8,128)S(1)} %prepare.1.parts, f32[8,128,256]{2,1,0:T(8,128)S(1)} %get-tuple-element.14.refs_1_.second, f32[8,128,256]{2,1,0:T(8,128)S(1)} %collective-permute-done.2.before, ...), custom_call_target="tpu_custom_call" | custom-call | flops 7864320 | bytes 23068672 | tf_op jit(solution)/shard_map/finish/pallas_call | solution.py:231
  42.5 0.9 fusion
  43.4 0.7 collective-permute-start.8
  44.1 4.3 %collective-permute-start.4 = (f32[4,128,256]{2,1,0:T(8,128)S(1)}, f32[4,128,256]{2,1,0:T(8,128)S(1)}, u32[]{:S(2)}, u32[]{:S(2)}) collective-permute-start(f32[4,128,256]{2,1,0:T(8,128)S(1)} %get-tuple-element.22), channel_id=1, source_target_pairs={{0,16},{16,32},{32,48},{48,64},{128,144},{144,160},{160,176},{176,... | collective-permute-start | bytes 1572872 | tf_op jit(solution)/shard_map/ppermute | solution.py:355
  48.4 0.0 collective-permute-done.8.received
  48.5 0.1 hop_down.3
  48.5 1.3 collective-permute-start.9
  49.8 8.9 %collective-permute-done.4.received = f32[4,128,256]{2,1,0:T(8,128)S(1)} collective-permute-done((f32[4,128,256]{2,1,0:T(8,128)S(1)}, f32[4,128,256]{2,1,0:T(8,128)S(1)}, u32[]{:S(2)}, u32[]{:S(2)}) %collective-permute-start.4) | collective-permute-done | bytes 524320 | tf_op jit(solution)/shard_map/ppermute | solution.py:355
  58.7 0.1 hop_up.3
  58.8 5.5 %collective-permute-start.5 = (f32[4,128,256]{2,1,0:T(8,128)S(1)}, f32[4,128,256]{2,1,0:T(8,128)S(1)}, u32[]{:S(2)}, u32[]{:S(2)}) collective-permute-start(f32[4,128,256]{2,1,0:T(8,128)S(1)} %hop_up.3), channel_id=1, source_target_pairs={{0,16},{16,32},{32,48},{48,64},{64,80},{80,96},{96,112},{112,128},... | collective-permute-start | bytes 1572872 | tf_op jit(solution)/shard_map/ppermute | solution.py:366
  64.3 0.5 collective-permute-done.9.received
  64.8 0.1 hop_down.4
  64.8 1.3 collective-permute-start.10
  66.1 7.6 %collective-permute-done.5.received = f32[4,128,256]{2,1,0:T(8,128)S(1)} collective-permute-done((f32[4,128,256]{2,1,0:T(8,128)S(1)}, f32[4,128,256]{2,1,0:T(8,128)S(1)}, u32[]{:S(2)}, u32[]{:S(2)}) %collective-permute-start.5) | collective-permute-done | bytes 524320 | tf_op jit(solution)/shard_map/ppermute | solution.py:366
  73.7 0.1 hop_up.4
  73.8 4.9 %collective-permute-start.6 = (f32[4,128,256]{2,1,0:T(8,128)S(1)}, f32[4,128,256]{2,1,0:T(8,128)S(1)}, u32[]{:S(2)}, u32[]{:S(2)}) collective-permute-start(f32[4,128,256]{2,1,0:T(8,128)S(1)} %hop_up.4), channel_id=1, source_target_pairs={{0,16},{16,32},{32,48},{48,64},{64,80},{80,96},{96,112},{112,128},... | collective-permute-start | bytes 1572872 | tf_op jit(solution)/shard_map/ppermute | solution.py:366
  78.7 8.9 %collective-permute-start.12 = (f32[4,128,256]{2,1,0:T(8,128)}, f32[4,128,256]{2,1,0:T(8,128)S(1)}, u32[]{:S(2)}, u32[]{:S(2)}) collective-permute-start(f32[4,128,256]{2,1,0:T(8,128)} %get-tuple-element.21), channel_id=1, source_target_pairs={{496,416},{0,80},{497,417},{1,81},{498,418},{2,82},{499,419},{3,83... | collective-permute-start | bytes 1572872 | tf_op jit(solution)/shard_map/ppermute | solution.py:364
  87.6 0.9 broadcast_select_fusion.1
  88.5 1.3 collective-permute-start.13
  89.8 0.0 collective-permute-done.10.received
  89.8 0.1 hop_down.5
  89.9 0.0 collective-permute-done.6.received
  89.9 0.1 hop_up.5
  90.0 0.9 broadcast_select_fusion
  90.8 28.5 %collective-permute-start.14 = (f32[4,128,256]{2,1,0:T(8,128)}, f32[4,128,256]{2,1,0:T(8,128)S(1)}, u32[]{:S(2)}, u32[]{:S(2)}) collective-permute-start(f32[4,128,256]{2,1,0:T(8,128)} %broadcast_select_fusion), channel_id=1, source_target_pairs={{496,384},{0,112},{497,385},{1,113},{498,386},{2,114},{499,387},{3... | collective-permute-start | bytes 1572872 | tf_op jit(solution)/shard_map/ppermute | solution.py:370
  119.3 1.3 collective-permute-start.11
  120.6 5.4 %collective-permute-start.7 = (f32[4,128,256]{2,1,0:T(8,128)S(1)}, f32[4,128,256]{2,1,0:T(8,128)}, u32[]{:S(2)}, u32[]{:S(2)}) collective-permute-start(f32[4,128,256]{2,1,0:T(8,128)S(1)} %hop_up.5), channel_id=1, source_target_pairs={{0,16},{16,32},{32,48},{48,64},{64,80},{80,96},{96,112},{112,128},... | collective-permute-start | bytes 1572872 | tf_op jit(solution)/shard_map/ppermute | solution.py:366
  126.0 0.3 collective-permute-done.14.refs_2_
  126.3 4.2 %collective-permute-done.11.right = f32[4,128,256]{2,1,0:T(8,128)} collective-permute-done((f32[4,128,256]{2,1,0:T(8,128)S(1)}, f32[4,128,256]{2,1,0:T(8,128)}, u32[]{:S(2)}, u32[]{:S(2)}) %collective-permute-start.11) | collective-permute-done | bytes 524320 | tf_op jit(solution)/shard_map/ppermute | solution.py:368
  130.5 1.4 collective-permute-done.7.left
  131.9 1.8 %merge.1 = f32[4,4,128,64]{3,2,1,0:T(8,128)S(1)} custom-call(s32[1]{0:T(128)} %bitcast.upper, f32[4,128,256]{2,1,0:T(8,128)S(1)} %get-tuple-element.23.own, f32[4,128,256]{2,1,0:T(8,128)} %collective-permute-done.7.left, f32[4,128,256]{2,1,0:T(8,128)} %collective-permute-done.11.right, f32[4,128,256]{2,1,0:T(8,128)S(1)} %collective-permute-done.12.refs_0_, ...), custom_call_target="tpu_custom_call" | custom-call | flops 2621440 | bytes 4194304 | tf_op jit(solution)/shard_map/merge/pallas_call | solution.py:299
  133.7 0.3 copy.4
  134.0 13.7 %all_to_all.5 = f32[4,4,128,64]{2,3,1,0:T(8,128)S(1)} all-to-all(f32[4,4,128,64]{2,3,1,0:T(8,128)S(1)} %copy.4), channel_id=1, replica_groups={{0,128,256,384},{16,144,272,400},{32,160,288,416},{48,176,304,432},{64,..., dimensions={0} | all-to-all | bytes 1048576 | tf_op jit(solution)/shard_map/all_to_all | solution.py:375
  147.7 0.3 copy.5.images
  148.1 0.1 fold.1
  148.1 0.8 copy.6
  (8 shorter events, 0.0 us)
Async XLA Ops:
  5.7 27.0 %collective-permute-start.2 = (f32[8,128,256]{2,1,0:T(8,128)}, f32[8,128,256]{2,1,0:T(8,128)S(1)}, u32[]{:S(2)}, u32[]{:S(2)}) collective-permute-start(f32[8,128,256]{2,1,0:T(8,128)} %get-tuple-element.16.refs_3_), channel_id=1, source_target_pairs={{0,16},{16,32},{32,48},{48,64},{64,80},{80,96},{96,112},{112,128},... | collective-permute-start | bytes 3145736 | tf_op jit(solution)/shard_map/ppermute | solution.py:390
  10.1 10.6 %copy-start = (s32[8]{0:T(128)S(1)}, s32[8]{0:T(128)}, u32[]{:S(2)}) copy-start(s32[8]{0:T(128)} %constant.18.clone) | copy-start | bytes 100
  10.1 27.4 %collective-permute-start.3 = (f32[8,128,256]{2,1,0:T(8,128)}, f32[8,128,256]{2,1,0:T(8,128)}, u32[]{:S(2)}, u32[]{:S(2)}) collective-permute-start(f32[8,128,256]{2,1,0:T(8,128)} %get-tuple-element.13.refs_0_), channel_id=1, source_target_pairs={{16,0},{32,16},{48,32},{64,48},{80,64},{96,80},{112,96},{128,112},... | collective-permute-start | bytes 3145736 | tf_op jit(solution)/shard_map/ppermute | solution.py:391
  16.3 4.4 %collective-permute-start.1 = (f32[32,256]{1,0:T(8,128)S(1)}, f32[32,256]{1,0:T(8,128)S(1)}, u32[]{:S(2)}, u32[]{:S(2)}) collective-permute-start(f32[32,256]{1,0:T(8,128)S(1)} %pad_maximum_fusion.1), channel_id=1, source_target_pairs={{1,0},{2,1},{3,2},{4,3},{5,4},{6,5},{7,6},{8,7},{9,8},{10,9},{11,1... | collective-permute-start | bytes 98312 | tf_op jit(solution)/shard_map/ppermute | solution.py:398
  18.7 5.2 %collective-permute-start = (f32[32,256]{1,0:T(8,128)S(1)}, f32[32,256]{1,0:T(8,128)S(1)}, u32[]{:S(2)}, u32[]{:S(2)}) collective-permute-start(f32[32,256]{1,0:T(8,128)S(1)} %pad_maximum_fusion), channel_id=1, source_target_pairs={{0,1},{1,2},{2,3},{3,4},{4,5},{5,6},{6,7},{7,8},{8,9},{9,10},{10,1... | collective-permute-start | bytes 98312 | tf_op jit(solution)/shard_map/ppermute | solution.py:397
  43.4 5.0 %collective-permute-start.8 = (f32[4,128,256]{2,1,0:T(8,128)S(1)}, f32[4,128,256]{2,1,0:T(8,128)S(1)}, u32[]{:S(2)}, u32[]{:S(2)}) collective-permute-start(f32[4,128,256]{2,1,0:T(8,128)S(1)} %get-tuple-element.22), channel_id=1, source_target_pairs={{64,48},{80,64},{96,80},{112,96},{192,176},{208,192},{224,208},{24... | collective-permute-start | bytes 1572872 | tf_op jit(solution)/shard_map/ppermute | solution.py:356
  44.1 14.6 %collective-permute-start.4 = (f32[4,128,256]{2,1,0:T(8,128)S(1)}, f32[4,128,256]{2,1,0:T(8,128)S(1)}, u32[]{:S(2)}, u32[]{:S(2)}) collective-permute-start(f32[4,128,256]{2,1,0:T(8,128)S(1)} %get-tuple-element.22), channel_id=1, source_target_pairs={{0,16},{16,32},{32,48},{48,64},{128,144},{144,160},{160,176},{176,... | collective-permute-start | bytes 1572872 | tf_op jit(solution)/shard_map/ppermute | solution.py:355
  48.5 16.2 %collective-permute-start.9 = (f32[4,128,256]{2,1,0:T(8,128)S(1)}, f32[4,128,256]{2,1,0:T(8,128)S(1)}, u32[]{:S(2)}, u32[]{:S(2)}) collective-permute-start(f32[4,128,256]{2,1,0:T(8,128)S(1)} %hop_down.3), channel_id=1, source_target_pairs={{16,0},{32,16},{48,32},{64,48},{80,64},{96,80},{112,96},{128,112},... | collective-permute-start | bytes 1572872 | tf_op jit(solution)/shard_map/ppermute | solution.py:368
  58.8 14.9 %collective-permute-start.5 = (f32[4,128,256]{2,1,0:T(8,128)S(1)}, f32[4,128,256]{2,1,0:T(8,128)S(1)}, u32[]{:S(2)}, u32[]{:S(2)}) collective-permute-start(f32[4,128,256]{2,1,0:T(8,128)S(1)} %hop_up.3), channel_id=1, source_target_pairs={{0,16},{16,32},{32,48},{48,64},{64,80},{80,96},{96,112},{112,128},... | collective-permute-start | bytes 1572872 | tf_op jit(solution)/shard_map/ppermute | solution.py:366
  64.8 25.0 %collective-permute-start.10 = (f32[4,128,256]{2,1,0:T(8,128)S(1)}, f32[4,128,256]{2,1,0:T(8,128)S(1)}, u32[]{:S(2)}, u32[]{:S(2)}) collective-permute-start(f32[4,128,256]{2,1,0:T(8,128)S(1)} %hop_down.4), channel_id=1, source_target_pairs={{16,0},{32,16},{48,32},{64,48},{80,64},{96,80},{112,96},{128,112},... | collective-permute-start | bytes 1572872 | tf_op jit(solution)/shard_map/ppermute | solution.py:368
  73.8 16.1 %collective-permute-start.6 = (f32[4,128,256]{2,1,0:T(8,128)S(1)}, f32[4,128,256]{2,1,0:T(8,128)S(1)}, u32[]{:S(2)}, u32[]{:S(2)}) collective-permute-start(f32[4,128,256]{2,1,0:T(8,128)S(1)} %hop_up.4), channel_id=1, source_target_pairs={{0,16},{16,32},{32,48},{48,64},{64,80},{80,96},{96,112},{112,128},... | collective-permute-start | bytes 1572872 | tf_op jit(solution)/shard_map/ppermute | solution.py:366
  78.7 47.3 %collective-permute-start.12 = (f32[4,128,256]{2,1,0:T(8,128)}, f32[4,128,256]{2,1,0:T(8,128)S(1)}, u32[]{:S(2)}, u32[]{:S(2)}) collective-permute-start(f32[4,128,256]{2,1,0:T(8,128)} %get-tuple-element.21), channel_id=1, source_target_pairs={{496,416},{0,80},{497,417},{1,81},{498,418},{2,82},{499,419},{3,83... | collective-permute-start | bytes 1572872 | tf_op jit(solution)/shard_map/ppermute | solution.py:364
  88.5 37.5 %collective-permute-start.13 = (f32[4,128,256]{2,1,0:T(8,128)}, f32[4,128,256]{2,1,0:T(8,128)S(1)}, u32[]{:S(2)}, u32[]{:S(2)}) collective-permute-start(f32[4,128,256]{2,1,0:T(8,128)} %broadcast_select_fusion.1), channel_id=1, source_target_pairs={{496,400},{0,96},{497,401},{1,97},{498,402},{2,98},{499,403},{3,99... | collective-permute-start | bytes 1572872 | tf_op jit(solution)/shard_map/ppermute | solution.py:370
  90.8 35.4 %collective-permute-start.14 = (f32[4,128,256]{2,1,0:T(8,128)}, f32[4,128,256]{2,1,0:T(8,128)S(1)}, u32[]{:S(2)}, u32[]{:S(2)}) collective-permute-start(f32[4,128,256]{2,1,0:T(8,128)} %broadcast_select_fusion), channel_id=1, source_target_pairs={{496,384},{0,112},{497,385},{1,113},{498,386},{2,114},{499,387},{3... | collective-permute-start | bytes 1572872 | tf_op jit(solution)/shard_map/ppermute | solution.py:370
  119.3 11.2 %collective-permute-start.11 = (f32[4,128,256]{2,1,0:T(8,128)S(1)}, f32[4,128,256]{2,1,0:T(8,128)}, u32[]{:S(2)}, u32[]{:S(2)}) collective-permute-start(f32[4,128,256]{2,1,0:T(8,128)S(1)} %hop_down.5), channel_id=1, source_target_pairs={{16,0},{32,16},{48,32},{64,48},{80,64},{96,80},{112,96},{128,112},... | collective-permute-start | bytes 1572872 | tf_op jit(solution)/shard_map/ppermute | solution.py:368
  120.6 11.2 %collective-permute-start.7 = (f32[4,128,256]{2,1,0:T(8,128)S(1)}, f32[4,128,256]{2,1,0:T(8,128)}, u32[]{:S(2)}, u32[]{:S(2)}) collective-permute-start(f32[4,128,256]{2,1,0:T(8,128)S(1)} %hop_up.5), channel_id=1, source_target_pairs={{0,16},{16,32},{32,48},{48,64},{64,80},{80,96},{96,112},{112,128},... | collective-permute-start | bytes 1572872 | tf_op jit(solution)/shard_map/ppermute | solution.py:366
